TPU v7x, 32 devices: a whole 2x2x4 slice. The times are simulated.
32 devices in a mesh: dp: 16 (over z, x, core), axial: 2 (over y).
Axes of the slice: x: 2, y: 2, z: 4, core: 2. Of those that a mesh axis runs over, the one named last changes fastest.
Arguments:
- homolog_activations: bfloat16 [16, 32, 16, 256], P('dp', None, 'axial'), may hold values from -6 to 6
- homolog_adjoint: bfloat16 [16, 32, 16, 256], P('dp', None, 'axial'), may hold values from -6 to 6
- duplex_adjoint: bfloat16 [16, 16, 16, 128], P('dp', 'axial'), may hold values from -6 to 6
- homolog_exists_filter: int32 [16, 32], P('dp'), may hold values 0 or 1
- amino_exists_filter: int32 [16, 16], P('dp'), may hold values 0 or 1
- focus_matrices_tier: bfloat16 [5, 256, 256], replicated, may hold values from -0.375 to 0.375
- affine_parameters: float32 [5, 256], replicated, may hold values from -1.5 to 1.75, as said below
- left_right_matrices: bfloat16 [256, 64], replicated, may hold values from -0.375 to 0.375
- outer_final_matrix: bfloat16 [1024, 128], replicated, may hold values from -0.1875 to 0.1875
Outputs:
- homolog_derivative: bfloat16 [16, 32, 16, 256], P('dp', None, 'axial')
- grad_attention: float32 [5, 256, 256], replicated
- grad_vectors: float32 [5, 256], replicated
- grad_proj: float32 [256, 64], replicated
- pair_weight_gradient: float32 [1024, 128], replicated
Inputs may be any that keep to these rules, and one draw needn't show every extreme that they name: `affine_parameters`: gains near one, biases near zero.
All inputs are finite; a program needn't handle non-finite values. No bound on the sum of `homolog_exists_filter` or of `amino_exists_filter` on one device may be relied on, other than what follows from the above.
Results may differ from a plain program's by a relative error of at most 0.018.
Values may be sent and summed in bfloat16 or wider, within the bound.
No kernel may reach another device: no remote copies, remote signals or barrier semaphores. Data moves between devices by JAX's collectives and lax.ppermute only.
A program may use at most 64 MiB of HBM per device.

v0:
```python
from functools import partial
import jax
import jax.numpy as jnp
from jax import lax
from jax.sharding import PartitionSpec as P

HEADS = 8
HEAD_DIM = 32
OUTER_FACTORS = 32
DUPLEX_FEATURES = 128


def layer_normalize(values, scale_row, shift_row):
    average = jnp.mean(values, axis=-1, keepdims=True)
    centered = values - average
    spread = jnp.mean(centered * centered, axis=-1, keepdims=True)
    return centered * lax.rsqrt(spread + 1e-05) * scale_row + shift_row


def column_attention_block(
    sequence_flags,
    residue_flags,
    alignment_block,
    focus_matrices_tier,
    affine_parameters,
    left_right_matrices,
):
    sequence_total, present_row_count, channel_width = alignment_block.shape
    normalized_input = layer_normalize(
        alignment_block.astype(jnp.float32), affine_parameters[0], affine_parameters[1]
    ).astype(jnp.bfloat16)
    flat_rows = normalized_input.reshape(sequence_total * present_row_count, channel_width)
    shape_heads = (sequence_total, present_row_count, HEADS, HEAD_DIM)
    queries = (
        (
            jnp.dot(flat_rows, focus_matrices_tier[0], preferred_element_type=jnp.float32)
            * HEAD_DIM ** (-0.5)
        )
        .astype(jnp.bfloat16)
        .reshape(shape_heads)
    )
    keys_all = (
        jnp.dot(flat_rows, focus_matrices_tier[1], preferred_element_type=jnp.float32)
        .astype(jnp.bfloat16)
        .reshape(shape_heads)
    )
    values_all = (
        jnp.dot(flat_rows, focus_matrices_tier[2], preferred_element_type=jnp.float32)
        .astype(jnp.bfloat16)
        .reshape(shape_heads)
    )
    gate_value = jax.nn.sigmoid(
        jnp.dot(flat_rows, focus_matrices_tier[3], preferred_element_type=jnp.float32)
        + affine_parameters[2]
    )
    logits = jnp.einsum("srhd,trhd->rhst", queries, keys_all, preferred_element_type=jnp.float32)
    mask_bias = (sequence_flags.astype(jnp.float32) - 1.0) * 1000000000.0
    probs = jax.nn.softmax(logits + mask_bias[None, None, None, :], axis=-1).astype(jnp.bfloat16)
    attended = jnp.einsum("rhst,trhd->srhd", probs, values_all, preferred_element_type=jnp.float32)
    gated = (
        attended.reshape(sequence_total * present_row_count, channel_width) * gate_value
    ).astype(jnp.bfloat16)
    rows_update = jnp.dot(gated, focus_matrices_tier[4], preferred_element_type=jnp.float32)
    updated_alignment = alignment_block.astype(jnp.float32) + rows_update.reshape(
        sequence_total, present_row_count, channel_width
    )
    second = (
        layer_normalize(updated_alignment, affine_parameters[3], affine_parameters[4])
        .astype(jnp.bfloat16)
        .reshape(sequence_total * present_row_count, channel_width)
    )
    projected = jnp.dot(second, left_right_matrices, preferred_element_type=jnp.float32).reshape(
        sequence_total, present_row_count, 2 * OUTER_FACTORS
    )
    flags = (sequence_flags[:, None] * residue_flags[None, :]).astype(jnp.float32)
    projected = (projected * flags[:, :, None]).astype(jnp.bfloat16)
    return (updated_alignment, projected[:, :, :OUTER_FACTORS], projected[:, :, OUTER_FACTORS:])


def pair_block(left_part, right_part, outer_final_matrix, flags_rows, flags_cols, seq_total):
    outer = jnp.einsum("sic,sje->ijce", left_part, right_part, precision=lax.Precision.HIGHEST)
    rows_i, cols_j = (outer.shape[0], outer.shape[1])
    outer_flat = outer.reshape(rows_i * cols_j, OUTER_FACTORS * OUTER_FACTORS).astype(jnp.bfloat16)
    pair_rows = jnp.dot(outer_flat, outer_final_matrix, preferred_element_type=jnp.float32).reshape(
        rows_i, cols_j, DUPLEX_FEATURES
    )
    divisor = jnp.maximum(flags_rows[:, None] * flags_cols[None, :] * seq_total, 1.0)
    return pair_rows / divisor[:, :, None]


def per_device(
    homolog_activations,
    homolog_adjoint,
    duplex_adjoint,
    homolog_exists_filter,
    amino_exists_filter,
    focus_matrices_tier,
    affine_parameters,
    left_right_matrices,
    outer_final_matrix,
):
    shard_homologs = homolog_activations[0]
    local_cotangent = homolog_adjoint[0]
    pair_update_cotangent = duplex_adjoint[0]
    sequence_flags = homolog_exists_filter[0]
    residue_flags = amino_exists_filter[0]
    present_row_count = shard_homologs.shape[1]
    own_index = lax.axis_index("axial")
    own_flags = lax.dynamic_slice_in_dim(
        residue_flags, own_index * present_row_count, present_row_count
    )
    seq_total = jnp.sum(sequence_flags.astype(jnp.float32))
    res_float = residue_flags.astype(jnp.float32)
    own_float = own_flags.astype(jnp.float32)
    local_function = partial(column_attention_block, sequence_flags, own_flags)
    step_outputs, backward_function = jax.vjp(
        local_function, shard_homologs, focus_matrices_tier, affine_parameters, left_right_matrices
    )
    left_own, right_own = lax.optimization_barrier((step_outputs[1], step_outputs[2]))
    left_float = left_own.astype(jnp.float32)
    right_all = lax.all_gather(right_own, "axial", axis=1, tiled=True)

    def pair_fn(left_part, right_part, weight_part):
        return pair_block(left_part, right_part, weight_part, own_float, res_float, seq_total)

    unused, back_pair = jax.vjp(
        pair_fn, left_float, right_all.astype(jnp.float32), outer_final_matrix
    )
    left_cot, right_cot, pair_weight_cot = back_pair(pair_update_cotangent.astype(jnp.float32))
    right_grad = lax.psum_scatter(
        right_cot.astype(jnp.bfloat16), "axial", scatter_dimension=1, tiled=True
    )
    pair_weight_gradient = pair_weight_cot.astype(jnp.float32)
    cotangent_list = (
        local_cotangent.astype(jnp.float32),
        left_cot.astype(jnp.bfloat16),
        right_grad,
    )
    alignment_piece, attention_piece, vector_piece, projection_piece = backward_function(
        cotangent_list
    )
    focus_derivative = attention_piece.astype(jnp.float32)
    affine_derivative = vector_piece
    factor_derivative = projection_piece.astype(jnp.float32)
    focus_derivative, affine_derivative, factor_derivative, pair_weight_gradient = lax.psum(
        (focus_derivative, affine_derivative, factor_derivative, pair_weight_gradient),
        ("dp", "axial"),
    )
    return (
        alignment_piece[None],
        focus_derivative,
        affine_derivative,
        factor_derivative,
        pair_weight_gradient,
    )


def solution(mesh):
    return jax.shard_map(
        per_device,
        mesh=mesh,
        in_specs=(
            P("dp", None, "axial", None),
            P("dp", None, "axial", None),
            P("dp", "axial", None, None),
            P("dp", None),
            P("dp", None),
            P(),
            P(),
            P(),
            P(),
        ),
        out_specs=(P("dp", None, "axial", None), P(), P(), P(), P()),
        check_vma=False,
    )
```

profile of v0, /device:TPU:0, one launch (start us, length us, event | category | flops | bytes accessed | tf_op | source)
XLA Modules:
  0.0 220.5 jit_solution(12519017308732594654)
XLA Ops:
  7.2 1.1 convert_reduce_fusion
  8.3 1.1 fusion.48
  9.4 1.5 fusion.131
  10.9 1.2 fusion.11
  12.1 1.2 convolution_convert_fusion.18
  13.4 1.2 convolution_convert_fusion.19
  15.1 0.7 add_multiply_fusion
  16.1 0.8 fusion.133
  17.2 0.3 copy-done.23
  17.5 0.6 copy-done.33
  18.1 0.6 convolution_bitcast_fusion
  18.7 0.9 copy.86
  19.6 0.3 reshape.445
  20.0 0.4 copy-done.39
  20.4 1.9 multiply_convert_fusion
  22.3 1.2 fusion.134
  24.2 0.4 copy-done.50
  24.9 0.7 fusion.130
  25.9 0.7 multiply_maximum_fusion.1
  26.9 0.8 reshape.446
  27.7 0.3 fusion.15
  28.0 0.8 reshape.467
  28.9 0.6 copy.88
  29.5 1.4 multiply_divide_fusion
  30.9 2.0 multiply_maximum_fusion
  32.9 6.3 %all_gather.3 = bf16[32,16,32]{2,1,0:T(8,128)(2,1)S(1)} all-gather(bf16[32,8,32]{2,1,0:T(8,128)(2,1)} %get-tuple-element.8), channel_id=1, replica_groups=mesh['dp'=16,'axial'=2] {'axial'}, dimensions={1}, use_global_device_ids=true | all-gather | bytes 49152 | tf_op jit(solution)/shard_map/all_gather | solution.py:121
  39.3 0.7 copy-done.10
  39.9 2.3 %fusion = bf16[8,16,32,32]{2,3,0,1:T(8,128)(2,1)} fusion(bf16[32,16,32,1]{2,1,0,3:T(8,128)(2,1)S(1)} %bitcast.263, bf16[32,8,32]{2,1,0:T(8,128)(2,1)} %copy-done.18), kind=kOutput, calls=%fused_computation.1 | convolution fusion | flops 8519680 | bytes 311296 | tf_op jit(solution)/shard_map/jvp(sic,sje->ijce)/dot_general | solution.py:81
  42.2 1.6 copy.105
  43.8 1.8 convert_element_type.291
  45.6 0.9 broadcast_divide_fusion
  46.5 2.0 fusion.6
  48.5 1.4 convolution_bitcast_fusion.2
  50.0 0.6 div.102
  50.7 0.8 reshape.468
  51.7 0.8 fusion.69
  52.9 1.8 fusion.135
  55.0 0.6 copy.94
  55.6 1.2 fusion.4
  56.8 0.6 fusion.31
  57.5 0.4 copy-done.5
  57.9 1.5 fusion.5
  59.4 1.5 fusion.3
  60.9 1.2 fusion.126
  62.1 1.9 copy.96
  64.0 0.4 reshape.450
  64.4 0.9 convolution_convert_fusion.16
  65.3 1.2 copy.99
  66.5 0.4 reshape.451
  66.9 0.9 convolution_convert_fusion.15
  68.1 0.4 mul.340
  68.7 1.4 fusion.51
  70.3 1.0 fusion.27
  71.6 0.3 fusion.23
  71.9 0.3 fusion.24
  72.3 0.3 fusion.22
  72.8 0.3 fusion.21
  73.1 1.2 add_convert_fusion
  75.0 41.5 %psum.29 = f32[5,256]{1,0:T(8,128)} all-reduce(f32[5,256]{1,0:T(8,128)S(1)} %pad_add_fusion.3), channel_id=1, replica_groups=mesh['dp'=16,'axial'=2] {'dp','axial'}, use_global_device_ids=true, to_apply=%region_19.0 | all-reduce | flops 1280 | bytes 10240 | tf_op jit(solution)/shard_map/psum | solution.py:145
  116.4 0.9 fusion.73
  117.3 92.3 %all-reduce.15.cloned.1.call-done = (f32[5,256,256]{2,1,0:T(8,128)}, f32[256,64]{0,1:T(8,128)}, f32[1024,128]{1,0:T(8,128)}) async-done(((f32[5,256,256]{2,1,0:T(8,128)}, f32[256,64]{0,1:T(8,128)}, f32[1024,128]{1,0:T(8,128)}), (f32[5,256,256]{2,1,0:T(8,128)}, f32[256,64]{0,1:T(8,128)}, f32[1024,128]{1,0:T(8,128)})) %all-reduce.15.cloned.1.call-update) | async-done | bytes 1900560 | tf_op jit(solution)/shard_map/psum | solution.py:145
  209.7 2.6 %copy.154 = f32[5,256,256]{2,1,0:T(8,128)} copy(f32[5,256,256]{2,1,0:T(8,128)} %get-tuple-element.52) | data formatting | bytes 2621440
  212.2 0.6 copy.155
  212.9 0.8 copy.156
  (192 shorter events, 4.9 us)
Async XLA Ops:
  7.2 19.5 %copy-start = (bf16[1024,128]{1,0:T(8,128)(2,1)S(1)}, bf16[1024,128]{1,0:T(8,128)(2,1)}, u32[]{:S(2)}) copy-start(bf16[1024,128]{1,0:T(8,128)(2,1)} %param.17) | copy-start | bytes 786436
  7.2 6.2 %copy-start.1 = (bf16[1,32,8,256]{3,2,1,0:T(8,128)(2,1)S(1)}, bf16[1,32,8,256]{3,2,1,0:T(8,128)(2,1)}, u32[]{:S(2)}) copy-start(bf16[1,32,8,256]{3,2,1,0:T(8,128)(2,1)} %param.9) | copy-start | bytes 393220
  7.2 43.5 %reduce-scatter.4.cloned.1.call-start = ((), (), s32[]{:S(2)}) async-start(), calls=%async_computation.1 | async-start | bytes 49152
  9.4 5.2 %copy-start.27 = (f32[32,8]{1,0:T(8,128)}, f32[32,8]{1,0:T(8,128)S(1)}, u32[]{:S(2)}) copy-start(f32[32,8]{1,0:T(8,128)S(1)} %fusion.48) | copy-start | bytes 3076
  9.4 5.4 %copy-start.38 = (f32[32,8]{1,0:T(8,128)}, f32[32,8]{1,0:T(8,128)S(1)}, u32[]{:S(2)}) copy-start(f32[32,8]{1,0:T(8,128)S(1)} %fusion.115) | copy-start | bytes 3076
  10.9 3.9 %copy-start.53 = (f32[1,256]{1,0:T(1,128)}, f32[1,256]{1,0:T(1,128)S(1)}, u32[]{:S(2)}) copy-start(f32[1,256]{1,0:T(1,128)S(1)} %get-tuple-element.31) | copy-start | bytes 3076
  10.9 3.9 %copy-start.65 = (f32[1,256]{1,0:T(1,128)}, f32[1,256]{1,0:T(1,128)S(1)}, u32[]{:S(2)}) copy-start(f32[1,256]{1,0:T(1,128)S(1)} %get-tuple-element.30) | copy-start | bytes 3076
  12.1 3.0 %copy-start.72 = (s32[1,32]{1,0:T(1,128)S(1)}, s32[1,32]{1,0:T(1,128)}, u32[]{:S(2)}) copy-start(s32[1,32]{1,0:T(1,128)} %param.12) | copy-start | bytes 388
  14.8 2.1 copy-start.4
  15.1 1.8 copy-start.6
  20.0 3.8 %copy-start.12 = (f32[256,256]{1,0:T(8,128)}, f32[256,256]{1,0:T(8,128)S(1)}, u32[]{:S(2)}) copy-start(f32[256,256]{1,0:T(8,128)S(1)} %reshape.445) | copy-start | bytes 786436
  20.3 3.4 %copy-start.74 = (s32[1,16]{1,0:T(1,128)S(1)}, s32[1,16]{1,0:T(1,128)}, u32[]{:S(2)}) copy-start(s32[1,16]{1,0:T(1,128)} %param.13) | copy-start | bytes 196
  20.3 3.5 %copy-start.73 = (s32[1,32]{1,0:T(1,128)S(1)}, s32[1,32]{1,0:T(1,128)}, u32[]{:S(2)}) copy-start(s32[1,32]{1,0:T(1,128)} %param.12) | copy-start | bytes 388
  20.3 4.3 %copy-start.58 = (f32[1,256]{1,0:T(1,128)S(1)}, f32[1,256]{1,0:T(1,128)}, u32[]{:S(2)}) copy-start(f32[1,256]{1,0:T(1,128)} %get-tuple-element.28) | copy-start | bytes 3076
  20.4 4.3 %copy-start.68 = (f32[1,256]{1,0:T(1,128)S(1)}, f32[1,256]{1,0:T(1,128)}, u32[]{:S(2)}) copy-start(f32[1,256]{1,0:T(1,128)} %get-tuple-element.32) | copy-start | bytes 3076
  20.4 4.3 %copy-start.75 = (bf16[256,64]{0,1:T(8,128)(2,1)S(1)}, bf16[256,64]{0,1:T(8,128)(2,1)}, u32[]{:S(2)}) copy-start(bf16[256,64]{0,1:T(8,128)(2,1)} %param.16) | copy-start | bytes 98308
  22.3 4.4 %copy-start.21 = (bf16[256,256]{1,0:T(8,128)(2,1)}, bf16[256,256]{1,0:T(8,128)(2,1)S(1)}, u32[]{:S(2)}) copy-start(bf16[256,256]{1,0:T(8,128)(2,1)S(1)} %get-tuple-element.39) | copy-start | bytes 393220
  22.3 4.3 %copy-start.36 = (bf16[1,8,16,128]{3,2,1,0:T(8,128)(2,1)S(1)}, bf16[1,8,16,128]{3,2,1,0:T(8,128)(2,1)}, u32[]{:S(2)}) copy-start(bf16[1,8,16,128]{3,2,1,0:T(8,128)(2,1)} %param.11) | copy-start | bytes 98308
  23.5 3.2 %copy-start.2 = (f32[32,8,256]{2,1,0:T(8,128)}, f32[32,8,256]{2,1,0:T(8,128)S(1)}, u32[]{:S(2)}) copy-start(f32[32,8,256]{2,1,0:T(8,128)S(1)} %get-tuple-element.42) | copy-start | bytes 786436
  23.7 2.9 %copy-start.25 = (f32[32,8]{1,0:T(8,128)}, f32[32,8]{1,0:T(8,128)S(1)}, u32[]{:S(2)}) copy-start(f32[32,8]{1,0:T(8,128)S(1)} %multiply_reduce_fusion.1) | copy-start | bytes 3076
  23.7 2.1 copy-start.46
  23.8 3.9 %copy-start.64 = (f32[16]{0:T(128)}, f32[16]{0:T(128)S(1)}, u32[]{:S(2)}) copy-start(f32[16]{0:T(128)S(1)} %convert_bitcast_fusion.2) | copy-start | bytes 196
  23.9 2.0 copy-start.57
  25.6 3.2 %copy-start.18 = (bf16[32,8,32]{2,1,0:T(8,128)(2,1)}, bf16[32,8,32]{2,1,0:T(8,128)(2,1)S(1)}, u32[]{:S(2)}) copy-start(bf16[32,8,32]{2,1,0:T(8,128)(2,1)S(1)} %get-tuple-element.7) | copy-start | bytes 49156
  28.9 180.8 %all-reduce.15.cloned.1.call-start = ((), (), s32[]{:S(2)}) async-start(), calls=%async_computation.2 | async-start | bytes 3801088 | tf_op jit(solution)/shard_map/psum | solution.py:145
  45.6 6.0 %copy-start.3 = (f32[32,8,256]{2,1,0:T(8,128)S(1)}, f32[32,8,256]{2,1,0:T(8,128)}, u32[]{:S(2)}) copy-start(f32[32,8,256]{2,1,0:T(8,128)} %copy-done.2) | copy-start | bytes 786436
  45.6 6.0 %copy-start.30 = (f32[32,8]{1,0:T(8,128)S(1)}, f32[32,8]{1,0:T(8,128)}, u32[]{:S(2)}) copy-start(f32[32,8]{1,0:T(8,128)} %copy-done.29) | copy-start | bytes 3076
  45.6 6.0 %copy-start.47 = (f32[32,8]{1,0:T(8,128)S(1)}, f32[32,8]{1,0:T(8,128)}, u32[]{:S(2)}) copy-start(f32[32,8]{1,0:T(8,128)} %copy-done.46) | copy-start | bytes 3076
  45.6 6.0 %copy-start.51 = (f32[32,8]{1,0:T(8,128)S(1)}, f32[32,8]{1,0:T(8,128)}, u32[]{:S(2)}) copy-start(f32[32,8]{1,0:T(8,128)} %copy-done.50) | copy-start | bytes 3076
  45.6 6.0 %copy-start.59 = (f32[1,256]{1,0:T(1,128)S(1)}, f32[1,256]{1,0:T(1,128)}, u32[]{:S(2)}) copy-start(f32[1,256]{1,0:T(1,128)} %get-tuple-element.28) | copy-start | bytes 3076
  45.6 6.0 %copy-start.76 = (bf16[256,64]{0,1:T(8,128)(2,1)S(1)}, bf16[256,64]{0,1:T(8,128)(2,1)}, u32[]{:S(2)}) copy-start(bf16[256,64]{0,1:T(8,128)(2,1)} %param.16) | copy-start | bytes 98308
  48.5 4.0 %copy-start.26 = (f32[32,8]{1,0:T(8,128)S(1)}, f32[32,8]{1,0:T(8,128)}, u32[]{:S(2)}) copy-start(f32[32,8]{1,0:T(8,128)} %copy-done.25) | copy-start | bytes 3076
  48.5 4.0 %copy-start.48 = (f32[32,8]{1,0:T(8,128)S(1)}, f32[32,8]{1,0:T(8,128)}, u32[]{:S(2)}) copy-start(f32[32,8]{1,0:T(8,128)} %copy-done.46) | copy-start | bytes 3076
  48.5 4.0 %copy-start.60 = (f32[1,256]{1,0:T(1,128)S(1)}, f32[1,256]{1,0:T(1,128)}, u32[]{:S(2)}) copy-start(f32[1,256]{1,0:T(1,128)} %get-tuple-element.28) | copy-start | bytes 3076
  50.0 2.9 %copy-start.11 = (bf16[1,32,8,256]{3,2,1,0:T(8,128)(2,1)S(1)}, bf16[1,32,8,256]{3,2,1,0:T(8,128)(2,1)}, u32[]{:S(2)}) copy-start(bf16[1,32,8,256]{3,2,1,0:T(8,128)(2,1)} %param.10) | copy-start | bytes 393220
  50.0 2.9 %copy-start.14 = (f32[256,256]{1,0:T(8,128)S(1)}, f32[256,256]{1,0:T(8,128)}, u32[]{:S(2)}) copy-start(f32[256,256]{1,0:T(8,128)} %get-tuple-element.40) | copy-start | bytes 786436
  50.7 2.1 copy-start.41
  52.9 2.7 %copy-start.24 = (f32[8,8,32]{2,1,0:T(8,128)S(1)}, f32[8,8,32]{2,1,0:T(8,128)}, u32[]{:S(2)}) copy-start(f32[8,8,32]{2,1,0:T(8,128)} %copy-done.23) | copy-start | bytes 24580
  52.9 2.7 %copy-start.34 = (f32[8,8,32]{2,1,0:T(8,128)S(1)}, f32[8,8,32]{2,1,0:T(8,128)}, u32[]{:S(2)}) copy-start(f32[8,8,32]{2,1,0:T(8,128)} %copy-done.33) | copy-start | bytes 24580
  55.6 1.2 copy-start.9
  55.6 1.2 copy-start.32
  57.9 1.5 copy-start.7
  59.4 1.5 copy-start.13
  59.4 1.5 copy-start.15
  59.4 1.5 copy-start.16
  60.9 3.5 %copy-start.17 = (bf16[5,256,256]{2,1,0:T(8,128)(2,1)S(1)}, bf16[5,256,256]{2,1,0:T(8,128)(2,1)}, u32[]{:S(2)}) copy-start(bf16[5,256,256]{2,1,0:T(8,128)(2,1)} %param.14) | copy-start | bytes 1966084
  64.4 3.4 %copy-start.20 = (bf16[32,8,8,32]{3,0,2,1:T(8,128)(2,1)S(1)}, bf16[32,8,8,32]{3,0,2,1:T(8,128)(2,1)}, u32[]{:S(2)}) copy-start(bf16[32,8,8,32]{3,0,2,1:T(8,128)(2,1)} %fusion.3) | copy-start | bytes 393220
  66.9 1.8 copy-start.40
  66.9 1.8 copy-start.55
  68.0 2.1 copy-start.28
  68.0 2.2 %copy-start.31 = (f32[32,8]{1,0:T(8,128)S(1)}, f32[32,8]{1,0:T(8,128)}, u32[]{:S(2)}) copy-start(f32[32,8]{1,0:T(8,128)} %copy-done.29) | copy-start | bytes 3076
  68.0 2.2 %copy-start.42 = (bf16[32,8,32]{2,1,0:T(8,128)(2,1)S(1)}, bf16[32,8,32]{2,1,0:T(8,128)(2,1)}, u32[]{:S(2)}) copy-start(bf16[32,8,32]{2,1,0:T(8,128)(2,1)} %copy-done.41) | copy-start | bytes 49156
  68.0 2.2 %copy-start.44 = (bf16[32,8,32]{2,1,0:T(8,128)(2,1)S(1)}, bf16[32,8,32]{2,1,0:T(8,128)(2,1)}, u32[]{:S(2)}) copy-start(bf16[32,8,32]{2,1,0:T(8,128)(2,1)} %copy-done.43) | copy-start | bytes 49156
  68.0 2.2 %copy-start.49 = (f32[32,8]{1,0:T(8,128)S(1)}, f32[32,8]{1,0:T(8,128)}, u32[]{:S(2)}) copy-start(f32[32,8]{1,0:T(8,128)} %copy-done.46) | copy-start | bytes 3076
  68.1 2.2 %copy-start.52 = (f32[32,8]{1,0:T(8,128)S(1)}, f32[32,8]{1,0:T(8,128)}, u32[]{:S(2)}) copy-start(f32[32,8]{1,0:T(8,128)} %copy-done.50) | copy-start | bytes 3076
  68.1 2.2 %copy-start.61 = (f32[1,256]{1,0:T(1,128)S(1)}, f32[1,256]{1,0:T(1,128)}, u32[]{:S(2)}) copy-start(f32[1,256]{1,0:T(1,128)} %get-tuple-element.28) | copy-start | bytes 3076
  68.1 2.2 %copy-start.69 = (f32[1,256]{1,0:T(1,128)S(1)}, f32[1,256]{1,0:T(1,128)}, u32[]{:S(2)}) copy-start(f32[1,256]{1,0:T(1,128)} %get-tuple-element.32) | copy-start | bytes 3076
  68.4 2.8 %copy-start.22 = (bf16[256,256]{1,0:T(8,128)(2,1)S(1)}, bf16[256,256]{1,0:T(8,128)(2,1)}, u32[]{:S(2)}) copy-start(bf16[256,256]{1,0:T(8,128)(2,1)} %copy-done.21) | copy-start | bytes 393220
  68.7 2.9 %copy-start.56 = (f32[1,256]{1,0:T(1,128)S(1)}, f32[1,256]{1,0:T(1,128)}, u32[]{:S(2)}) copy-start(f32[1,256]{1,0:T(1,128)} %copy-done.53) | copy-start | bytes 3076
  68.7 2.9 %copy-start.67 = (f32[1,256]{1,0:T(1,128)S(1)}, f32[1,256]{1,0:T(1,128)}, u32[]{:S(2)}) copy-start(f32[1,256]{1,0:T(1,128)} %copy-done.65) | copy-start | bytes 3076
  71.3 1.5 copy-start.37
  71.3 1.5 copy-start.62
  209.7 2.6 %copy-start.45 = (f32[256,64]{0,1:T(8,128)S(1)}, f32[256,64]{0,1:T(8,128)}, u32[]{:S(2)}) copy-start(f32[256,64]{0,1:T(8,128)} %get-tuple-element.54) | copy-start | bytes 196612
  209.7 3.2 %copy-start.19 = (f32[1024,128]{1,0:T(8,128)S(1)}, f32[1024,128]{1,0:T(8,128)}, u32[]{:S(2)}) copy-start(f32[1024,128]{1,0:T(8,128)} %get-tuple-element.55) | copy-start | bytes 1572868
  (15 other events, 11.7 us)
Sparse Core Ops, SparseCore 0:
  29.0 12.4 reduce-scatter.3
  74.4 135.1 all-reduce.14
where the time goes:
time: 221 us
  waiting for transfers between devices  92.4 us (42%)
  blocking collectives  47.8 us (22%)
  matrix products  28.2 us (13%)
  local copies, waits for them, and re-layouts  24.5 us (11%)
  between operations  15.2 us (7%)
  other arithmetic  12.4 us (6%)
    psum x1, waiting for transfers between devices, per_device(): lax.psum((focus_derivative, affine_derivative, factor_derivative, pair_we...  92.3 us
    psum x1, blocking collectives, per_device(): lax.psum((focus_derivative, affine_derivative, factor_derivative, pair_we...  41.5 us
    unnamed x160, local copies, waits for them, and re-layouts  9.1 us
    all_gather x1, blocking collectives, per_device(): right_all = lax.all_gather(right_own, 'axial', axis=1, tiled=True)  6.33 us
  transfers between devices with their start and end apart: 2, of which 1 were waited for; matrix products, arithmetic and copies ran while one was open for 7% of the time, Pallas kernels for 0%

commit v1 on v0

--- a/solution.py
+++ b/solution.py
@@ -143,8 +143,10 @@
     affine_derivative = vector_piece
     factor_derivative = projection_piece.astype(jnp.float32)
     focus_derivative, affine_derivative, factor_derivative, pair_weight_gradient = lax.psum(
-        (focus_derivative, affine_derivative, factor_derivative, pair_weight_gradient),
-        ("dp", "axial"),
+        lax.psum(
+            (focus_derivative, affine_derivative, factor_derivative, pair_weight_gradient), "axial"
+        ),
+        "dp",
     )
     return (
         alignment_piece[None],

time: 221 us -> 249 us (1.13)
  waiting for transfers between devices: 92.4 us -> 121 us
    psum x0 -> x1, waiting for transfers between devices: none -> 61.1 us  [per_device(): lax.psum(lax.psum((focus_derivative, affine_derivative, factor_derivative...]
    psum x1, blocking collectives: 41.5 us -> 5.01 us  [per_device(): lax.psum((focus_derivative, affine_derivative, factor_derivative, pair_we...]
    psum x0 -> x1, blocking collectives: none -> 33.9 us  [per_device(): lax.psum(lax.psum((focus_derivative, affine_derivative, factor_derivative...]
    psum x1, waiting for transfers between devices: 92.3 us -> 59.4 us  [per_device(): lax.psum((focus_derivative, affine_derivative, factor_derivative, pair_we...]
    unnamed x160 -> x146, local copies, waits for them, and re-layouts: 9.1 us -> 6.9 us
  transfers between devices with their start and end apart: 2 -> 3, of which waited for: 1 -> 2; matrix products, arithmetic and copies ran while one was open for 7% -> 6% of each run, Pallas kernels for 0% -> 0%
where the time goes in v1:
time: 249 us; the launch traced here: 248 us
  waiting for transfers between devices  121 us (49%)
  blocking collectives  46.9 us (19%)
  matrix products  29.5 us (12%)
  local copies, waits for them, and re-layouts  23.1 us (9%)
  between operations  15 us (6%)
  other arithmetic  13.2 us (5%)
    psum x1, waiting for transfers between devices, per_device(): lax.psum(lax.psum((focus_derivative, affine_derivative, factor_derivative...  61.1 us
    psum x1, waiting for transfers between devices, per_device(): lax.psum((focus_derivative, affine_derivative, factor_derivative, pair_we...  59.4 us
    psum x1, blocking collectives, per_device(): lax.psum(lax.psum((focus_derivative, affine_derivative, factor_derivative...  33.9 us
    all_gather x1, blocking collectives, per_device(): right_all = lax.all_gather(right_own, 'axial', axis=1, tiled=True)  8.05 us
    unnamed x146, local copies, waits for them, and re-layouts  6.9 us
    psum x1, blocking collectives, per_device(): lax.psum((focus_derivative, affine_derivative, factor_derivative, pair_we...  5.01 us
  transfers between devices with their start and end apart: 3, of which 2 were waited for; matrix products, arithmetic and copies ran while one was open for 6% of the time, Pallas kernels for 0%

profile of v1, /device:TPU:0, one launch (start us, length us, event | category | flops | bytes accessed | tf_op | source)
XLA Modules:
  0.0 248.3 jit_solution(14809274938996863928)
XLA Ops:
  7.2 1.1 convert_reduce_fusion
  8.3 1.1 fusion.48
  9.5 0.9 fusion.131
  10.4 1.2 fusion.11
  11.6 1.2 convolution_convert_fusion.18
  12.9 1.2 convolution_convert_fusion.19
  14.6 0.7 add_multiply_fusion
  15.6 0.8 fusion.133
  16.4 0.3 fusion.36
  16.7 1.5 convolution_bitcast_fusion
  18.3 2.1 copy.86
  20.4 0.3 reshape.445
  20.8 2.0 multiply_convert_fusion
  22.8 1.2 fusion.134
  24.7 0.5 copy-done.51
  25.4 0.7 fusion.130
  26.4 0.6 multiply_maximum_fusion.1
  27.4 0.8 reshape.446
  28.2 0.4 fusion.15
  28.5 0.8 reshape.467
  29.4 0.6 copy.88
  30.0 1.4 multiply_divide_fusion
  31.4 1.9 multiply_maximum_fusion
  33.3 8.0 %all_gather.3 = bf16[32,16,32]{2,1,0:T(8,128)(2,1)} all-gather(bf16[32,8,32]{2,1,0:T(8,128)(2,1)} %get-tuple-element.8), channel_id=1, replica_groups=mesh['dp'=16,'axial'=2] {'axial'}, dimensions={1}, use_global_device_ids=true | all-gather | bytes 49152 | tf_op jit(solution)/shard_map/all_gather | solution.py:121
  41.4 2.3 fusion
  43.7 1.6 copy.105
  45.3 1.8 convert_element_type.291
  47.1 0.9 broadcast_divide_fusion
  48.0 2.0 fusion.6
  50.1 1.4 convolution_bitcast_fusion.2
  51.5 0.7 div.102
  52.3 0.8 reshape.468
  53.2 1.7 fusion.69
  54.9 1.0 fusion.128
  56.0 1.8 fusion.135
  58.1 0.6 copy.94
  58.8 2.0 fusion.4
  60.8 0.6 fusion.31
  61.5 0.4 copy-done.5
  61.9 1.5 fusion.5
  63.4 1.5 fusion.3
  64.9 1.3 fusion.126
  66.2 2.0 copy.96
  68.1 0.4 reshape.450
  68.7 1.2 copy.99
  70.0 0.4 reshape.451
  70.9 0.4 mul.340
  71.5 1.3 fusion.51
  73.0 1.0 fusion.27
  74.0 0.3 fusion.20
  74.3 0.3 fusion.23
  74.6 0.3 fusion.24
  75.0 0.3 fusion.22
  75.5 0.3 fusion.21
  75.8 1.2 add_convert_fusion
  77.1 59.4 %all-reduce.19.cloned.1.call-done = (f32[5,256,256]{2,1,0:T(8,128)}, f32[256,64]{0,1:T(8,128)}, f32[1024,128]{1,0:T(8,128)}) async-done(((f32[5,256,256]{2,1,0:T(8,128)}, f32[256,64]{0,1:T(8,128)}, f32[1024,128]{1,0:T(8,128)}), (f32[5,256,256]{2,1,0:T(8,128)}, f32[256,64]{0,1:T(8,128)}, f32[1024,128]{1,0:T(8,128)})) %all-reduce.19.cloned.1.call-update) | async-done | bytes 1900560 | tf_op jit(solution)/shard_map/psum | solution.py:146
  136.5 0.3 fusion.125
  136.9 5.0 %psum.58 = f32[5,256]{1,0:T(8,128)S(1)} all-reduce(f32[5,256]{1,0:T(8,128)S(1)} %pad_add_fusion.3), channel_id=1, replica_groups=mesh['dp'=16,'axial'=2] {'axial'}, use_global_device_ids=true, to_apply=%region_20.0 | all-reduce | flops 1280 | bytes 10240 | tf_op jit(solution)/shard_map/psum | solution.py:146
  141.9 33.9 %psum.59 = f32[5,256]{1,0:T(8,128)} all-reduce(f32[5,256]{1,0:T(8,128)S(1)} %psum.58), channel_id=1, replica_groups=mesh['dp'=16,'axial'=2] {'dp'}, use_global_device_ids=true, to_apply=%region_21.0 | all-reduce | flops 1280 | bytes 10240 | tf_op jit(solution)/shard_map/psum | solution.py:145
  175.8 0.9 fusion.73
  176.7 61.1 %all-reduce.17.cloned.1.call-done = (f32[5,256,256]{2,1,0:T(8,128)}, f32[256,64]{0,1:T(8,128)}, f32[1024,128]{1,0:T(8,128)}) async-done(((f32[5,256,256]{2,1,0:T(8,128)}, f32[256,64]{0,1:T(8,128)}, f32[1024,128]{1,0:T(8,128)}), (f32[5,256,256]{2,1,0:T(8,128)}, f32[256,64]{0,1:T(8,128)}, f32[1024,128]{1,0:T(8,128)})) %all-reduce.17.cloned.1.call-update) | async-done | bytes 1900560 | tf_op jit(solution)/shard_map/psum | solution.py:145
  237.8 2.6 %copy.157 = f32[5,256,256]{2,1,0:T(8,128)} copy(f32[5,256,256]{2,1,0:T(8,128)} %get-tuple-element.55) | data formatting | bytes 2621440
  240.4 0.6 copy.158
  241.0 0.8 copy.159
  (182 shorter events, 4.1 us)
Async XLA Ops:
  7.2 20.0 %copy-start = (bf16[1024,128]{1,0:T(8,128)(2,1)S(1)}, bf16[1024,128]{1,0:T(8,128)(2,1)}, u32[]{:S(2)}) copy-start(bf16[1024,128]{1,0:T(8,128)(2,1)} %param.17) | copy-start | bytes 786436
  7.2 5.7 %copy-start.1 = (bf16[1,32,8,256]{3,2,1,0:T(8,128)(2,1)S(1)}, bf16[1,32,8,256]{3,2,1,0:T(8,128)(2,1)}, u32[]{:S(2)}) copy-start(bf16[1,32,8,256]{3,2,1,0:T(8,128)(2,1)} %param.9) | copy-start | bytes 393220
  7.2 45.1 %reduce-scatter.4.cloned.1.call-start = ((), (), s32[]{:S(2)}) async-start(), calls=%async_computation.1 | async-start | bytes 49152
  8.3 43.2 %copy-start.27 = (f32[32,8]{1,0:T(8,128)}, f32[32,8]{1,0:T(8,128)S(1)}, u32[]{:S(2)}) copy-start(f32[32,8]{1,0:T(8,128)S(1)} %broadcast_multiply_fusion.1) | copy-start | bytes 3076
  9.4 4.6 %copy-start.31 = (f32[32,8]{1,0:T(8,128)}, f32[32,8]{1,0:T(8,128)S(1)}, u32[]{:S(2)}) copy-start(f32[32,8]{1,0:T(8,128)S(1)} %fusion.48) | copy-start | bytes 3076
  9.4 11.3 %copy-start.41 = (f32[32,8]{1,0:T(8,128)}, f32[32,8]{1,0:T(8,128)S(1)}, u32[]{:S(2)}) copy-start(f32[32,8]{1,0:T(8,128)S(1)} %fusion.115) | copy-start | bytes 3076
  10.3 10.4 %copy-start.53 = (f32[1,256]{1,0:T(1,128)}, f32[1,256]{1,0:T(1,128)S(1)}, u32[]{:S(2)}) copy-start(f32[1,256]{1,0:T(1,128)S(1)} %get-tuple-element.34) | copy-start | bytes 3076
  10.3 10.4 %copy-start.62 = (f32[1,256]{1,0:T(1,128)}, f32[1,256]{1,0:T(1,128)S(1)}, u32[]{:S(2)}) copy-start(f32[1,256]{1,0:T(1,128)S(1)} %get-tuple-element.33) | copy-start | bytes 3076
  10.4 14.2 %copy-start.57 = (f32[1,256]{1,0:T(1,128)}, f32[1,256]{1,0:T(1,128)S(1)}, u32[]{:S(2)}) copy-start(f32[1,256]{1,0:T(1,128)S(1)} %get-tuple-element.31) | copy-start | bytes 3076
  10.4 14.2 %copy-start.64 = (f32[1,256]{1,0:T(1,128)}, f32[1,256]{1,0:T(1,128)S(1)}, u32[]{:S(2)}) copy-start(f32[1,256]{1,0:T(1,128)S(1)} %get-tuple-element.35) | copy-start | bytes 3076
  11.6 2.9 %copy-start.67 = (s32[1,32]{1,0:T(1,128)S(1)}, s32[1,32]{1,0:T(1,128)}, u32[]{:S(2)}) copy-start(s32[1,32]{1,0:T(1,128)} %param.12) | copy-start | bytes 388
  14.3 2.1 copy-start.4
  14.6 1.9 copy-start.6
  16.4 1.9 copy-start.25
  16.7 1.6 copy-start.37
  20.7 3.5 %copy-start.12 = (f32[256,256]{1,0:T(8,128)}, f32[256,256]{1,0:T(8,128)S(1)}, u32[]{:S(2)}) copy-start(f32[256,256]{1,0:T(8,128)S(1)} %reshape.445) | copy-start | bytes 786436
  20.8 3.5 %copy-start.68 = (s32[1,16]{1,0:T(1,128)S(1)}, s32[1,16]{1,0:T(1,128)}, u32[]{:S(2)}) copy-start(s32[1,16]{1,0:T(1,128)} %param.13) | copy-start | bytes 196
  20.8 4.3 %copy-start.69 = (bf16[256,64]{0,1:T(8,128)(2,1)S(1)}, bf16[256,64]{0,1:T(8,128)(2,1)}, u32[]{:S(2)}) copy-start(bf16[256,64]{0,1:T(8,128)(2,1)} %param.16) | copy-start | bytes 98308
  22.8 4.3 %copy-start.23 = (bf16[256,256]{1,0:T(8,128)(2,1)}, bf16[256,256]{1,0:T(8,128)(2,1)S(1)}, u32[]{:S(2)}) copy-start(bf16[256,256]{1,0:T(8,128)(2,1)S(1)} %get-tuple-element.42) | copy-start | bytes 393220
  22.8 4.2 %copy-start.39 = (bf16[1,8,16,128]{3,2,1,0:T(8,128)(2,1)S(1)}, bf16[1,8,16,128]{3,2,1,0:T(8,128)(2,1)}, u32[]{:S(2)}) copy-start(bf16[1,8,16,128]{3,2,1,0:T(8,128)(2,1)} %param.11) | copy-start | bytes 98308
  24.0 3.1 %copy-start.2 = (f32[32,8,256]{2,1,0:T(8,128)}, f32[32,8,256]{2,1,0:T(8,128)S(1)}, u32[]{:S(2)}) copy-start(f32[32,8,256]{2,1,0:T(8,128)S(1)} %get-tuple-element.45) | copy-start | bytes 786436
  24.2 2.9 %copy-start.29 = (f32[32,8]{1,0:T(8,128)}, f32[32,8]{1,0:T(8,128)S(1)}, u32[]{:S(2)}) copy-start(f32[32,8]{1,0:T(8,128)S(1)} %multiply_reduce_fusion.1) | copy-start | bytes 3076
  24.2 2.1 copy-start.48
  24.3 2.0 copy-start.61
  24.4 2.0 copy-start.56
  26.1 2.4 copy-start.20
  29.3 107.1 %all-reduce.19.cloned.1.call-start = ((), (), s32[]{:S(2)}) async-start(), calls=%async_computation.3 | async-start | bytes 3801088 | tf_op jit(solution)/shard_map/psum | solution.py:146
  47.1 6.0 %copy-start.3 = (f32[32,8,256]{2,1,0:T(8,128)S(1)}, f32[32,8,256]{2,1,0:T(8,128)}, u32[]{:S(2)}) copy-start(f32[32,8,256]{2,1,0:T(8,128)} %copy-done.2) | copy-start | bytes 786436
  47.1 6.1 %copy-start.34 = (f32[32,8]{1,0:T(8,128)S(1)}, f32[32,8]{1,0:T(8,128)}, u32[]{:S(2)}) copy-start(f32[32,8]{1,0:T(8,128)} %copy-done.33) | copy-start | bytes 3076
  47.1 6.1 %copy-start.49 = (f32[32,8]{1,0:T(8,128)S(1)}, f32[32,8]{1,0:T(8,128)}, u32[]{:S(2)}) copy-start(f32[32,8]{1,0:T(8,128)} %copy-done.48) | copy-start | bytes 3076
  50.1 4.8 %copy-start.30 = (f32[32,8]{1,0:T(8,128)S(1)}, f32[32,8]{1,0:T(8,128)}, u32[]{:S(2)}) copy-start(f32[32,8]{1,0:T(8,128)} %copy-done.29) | copy-start | bytes 3076
  51.5 4.5 %copy-start.10 = (bf16[1,32,8,256]{3,2,1,0:T(8,128)(2,1)S(1)}, bf16[1,32,8,256]{3,2,1,0:T(8,128)(2,1)}, u32[]{:S(2)}) copy-start(bf16[1,32,8,256]{3,2,1,0:T(8,128)(2,1)} %param.10) | copy-start | bytes 393220
  51.5 4.5 %copy-start.16 = (f32[256,256]{1,0:T(8,128)S(1)}, f32[256,256]{1,0:T(8,128)}, u32[]{:S(2)}) copy-start(f32[256,256]{1,0:T(8,128)} %get-tuple-element.43) | copy-start | bytes 786436
  52.2 2.7 %copy-start.43 = (bf16[32,8,32]{2,1,0:T(8,128)(2,1)}, bf16[32,8,32]{2,1,0:T(8,128)(2,1)S(1)}, u32[]{:S(2)}) copy-start(bf16[32,8,32]{2,1,0:T(8,128)(2,1)S(1)} %copy.144) | copy-start | bytes 49156
  53.2 1.7 copy-start.45
  54.9 3.0 %copy-start.14 = (f32[256,256]{1,0:T(8,128)}, f32[256,256]{1,0:T(8,128)S(1)}, u32[]{:S(2)}) copy-start(f32[256,256]{1,0:T(8,128)S(1)} %get-tuple-element.46) | copy-start | bytes 786436
  58.7 2.1 copy-start.9
  58.7 2.1 copy-start.26
  58.7 2.1 copy-start.36
  61.9 1.5 copy-start.7
  63.3 1.5 copy-start.13
  63.4 1.5 copy-start.17
  63.4 1.5 copy-start.18
  66.1 2.3 copy-start.19
  68.5 2.1 copy-start.22
  70.8 2.0 copy-start.32
  70.8 2.1 copy-start.35
  70.8 2.1 copy-start.44
  70.8 2.1 copy-start.46
  70.8 2.1 copy-start.50
  70.9 2.1 copy-start.52
  70.9 2.1 copy-start.58
  70.9 2.1 copy-start.65
  71.2 2.7 %copy-start.11 = (bf16[1,32,8,256]{3,2,1,0:T(8,128)(2,1)S(1)}, bf16[1,32,8,256]{3,2,1,0:T(8,128)(2,1)}, u32[]{:S(2)}) copy-start(bf16[1,32,8,256]{3,2,1,0:T(8,128)(2,1)} %param.10) | copy-start | bytes 393220
  71.3 2.7 %copy-start.24 = (bf16[256,256]{1,0:T(8,128)(2,1)S(1)}, bf16[256,256]{1,0:T(8,128)(2,1)}, u32[]{:S(2)}) copy-start(bf16[256,256]{1,0:T(8,128)(2,1)} %copy-done.23) | copy-start | bytes 393220
  71.5 2.7 %copy-start.55 = (f32[1,256]{1,0:T(1,128)S(1)}, f32[1,256]{1,0:T(1,128)}, u32[]{:S(2)}) copy-start(f32[1,256]{1,0:T(1,128)} %copy-done.53) | copy-start | bytes 3076
  71.5 2.7 %copy-start.63 = (f32[1,256]{1,0:T(1,128)S(1)}, f32[1,256]{1,0:T(1,128)}, u32[]{:S(2)}) copy-start(f32[1,256]{1,0:T(1,128)} %copy-done.62) | copy-start | bytes 3076
  74.0 1.5 copy-start.59
  77.0 59.5 %copy-start.15 = (f32[256,256]{1,0:T(8,128)S(1)}, f32[256,256]{1,0:T(8,128)}, u32[]{:S(2)}) copy-start(f32[256,256]{1,0:T(8,128)} %copy-done.14) | copy-start | bytes 786436
  77.0 59.9 %copy-start.60 = (f32[256]{0:T(256)S(1)}, f32[256]{0:T(256)}, u32[]{:S(2)}) copy-start(f32[256]{0:T(256)} %get-tuple-element.21) | copy-start | bytes 3076
  77.0 59.9 %copy-start.66 = (f32[256]{0:T(256)S(1)}, f32[256]{0:T(256)}, u32[]{:S(2)}) copy-start(f32[256]{0:T(256)} %get-tuple-element.9) | copy-start | bytes 3076
  77.0 160.8 %all-reduce.17.cloned.1.call-start = ((), (), s32[]{:S(2)}) async-start(), calls=%async_computation.2 | async-start | bytes 3801088 | tf_op jit(solution)/shard_map/psum | solution.py:145
  237.8 2.6 %copy-start.47 = (f32[256,64]{0,1:T(8,128)S(1)}, f32[256,64]{0,1:T(8,128)}, u32[]{:S(2)}) copy-start(f32[256,64]{0,1:T(8,128)} %get-tuple-element.57) | copy-start | bytes 196612
  237.8 3.2 %copy-start.21 = (f32[1024,128]{1,0:T(8,128)S(1)}, f32[1024,128]{1,0:T(8,128)}, u32[]{:S(2)}) copy-start(f32[1024,128]{1,0:T(8,128)} %get-tuple-element.58) | copy-start | bytes 1572868
  (9 other events, 9.5 us)
Sparse Core Ops, SparseCore 0:
  29.4 12.4 reduce-scatter.3
  77.1 59.2 all-reduce.18
  140.7 97.0 all-reduce.16
